TPU v7x, 32 devices: a whole 2x2x4 slice. The times are simulated.
32 devices in a mesh: replica: 16 (over z, x, core), shard: 2 (over y).
Axes of the slice: x: 2, y: 2, z: 4, core: 2. Of those that a mesh axis runs over, the one named last changes fastest.
Arguments:
- frames: bfloat16 [32768, 768], P(('replica', 'shard')), may hold values from -6 to 6
- cotangent: bfloat16 [32768, 768], P(('replica', 'shard')), may hold values from -6 to 6
- segment_ids: int32 [32, 1024], P(('replica', 'shard')), may hold values from 0 to 7, never falling along the last dimension, each value on 1 to 512 neighbouring positions
- norm_gain: bfloat16 [2, 768], P(None, 'shard'), may hold values from 0.099609375 to 1.8984375
- norm_bias: bfloat16 [2, 768], P(None, 'shard'), may hold values from -2 to 2
- w_qkv: bfloat16 [768, 2304], P('shard'), may hold values from -0.21875 to 0.21875
- qv_bias: bfloat16 [2, 768], P(None, 'shard'), may hold values from -2 to 2
- w_out: bfloat16 [768, 768], P('shard'), may hold values from -0.875 to 0.875
- out_bias: bfloat16 [2, 768], P(None, 'shard'), may hold values from -2 to 2
- w_up: bfloat16 [768, 3072], P(None, 'shard'), may hold values from -0.21875 to 0.21875
- up_bias: bfloat16 [3072], P('shard'), may hold values from -3 to 3
- w_down: bfloat16 [3072, 768], P('shard'), may hold values from -0.109375 to 0.109375
Outputs:
- out_frames: bfloat16 [32768, 768], P(('replica', 'shard'))
- d_frames: float32 [32768, 768], P(('replica', 'shard'))
- d_norm_gain: float32 [2, 768], P(None, 'shard')
- d_norm_bias: float32 [2, 768], P(None, 'shard')
- d_w_qkv: float32 [768, 2304], P('shard')
- d_qv_bias: float32 [2, 768], P(None, 'shard')
- d_w_out: float32 [768, 768], P('shard')
- d_out_bias: float32 [2, 768], P(None, 'shard')
- d_w_up: float32 [768, 3072], P(None, 'shard')
- d_up_bias: float32 [3072], P('shard')
- d_w_down: float32 [3072, 768], P('shard')
Inputs may be any that keep to these rules, and one draw needn't show every extreme that they name: `segment_ids`: each row numbers the documents of one sequence in order: never falling, every number of 0 to 7 used, no document longer than 512 frames, and one exactly that long in every row.
All inputs are finite; a program needn't handle non-finite values.
Results may differ from a plain program's by a relative error of at most 0.018.
Values may be sent and summed in bfloat16 or wider, within the bound.
No kernel may reach another device: no remote copies, remote signals or barrier semaphores. Data moves between devices by JAX's collectives and lax.ppermute only.
A program may use at most 256 MiB of HBM per device.

v0:
```python
import math
import jax
import jax.numpy as jnp
from jax import lax
from jax.sharding import PartitionSpec as P

H = 12
EPS = 1e-05
NEG = -1e30


def standardize(values):
    centered = values - jnp.mean(values, axis=1, keepdims=True)
    inverse = lax.rsqrt(jnp.mean(centered * centered, axis=1, keepdims=True) + EPS)
    return (centered * inverse, inverse)


def norm_back(grad_unit, unit, inverse):
    return inverse * (
        grad_unit
        - jnp.mean(grad_unit, axis=1, keepdims=True)
        - unit * jnp.mean(grad_unit * unit, axis=1, keepdims=True)
    )


def gelu_exact(values):
    return jax.nn.gelu(values, approximate=False)


def gelu_back(values, gradient):
    _, pull = jax.vjp(gelu_exact, values)
    return pull(gradient)[0]


def halves(array, which, axis):
    size = array.shape[axis] // 2
    return lax.slice_in_dim(array, which * size, (which + 1) * size, axis=axis)


def touching(query_seg, key_seg):
    return jnp.logical_and(query_seg[-1] >= key_seg[0], query_seg[0] <= key_seg[-1])


def keep_same(carry):
    return carry


def masked_scores(query_part, key_part, query_seg, key_seg):
    scale = 1.0 / math.sqrt(query_part.shape[2])
    raw = (
        jnp.einsum("qhd,khd->hqk", query_part, key_part, preferred_element_type=jnp.float32) * scale
    )
    same = query_seg[:, None] == key_seg[None, :]
    return jnp.where(same[None], raw, NEG)


def attend_forward(packed):
    queries, key_rows, value_rows, segment = packed
    outputs = []
    norms = []
    for query_pos in range(2):
        query_part = halves(queries, query_pos, 0)
        query_seg = halves(segment, query_pos, 0)
        span, heads, head_dim = query_part.shape
        peak = jnp.full((heads, span), NEG, jnp.float32)
        mass = jnp.zeros((heads, span), jnp.float32)
        for key_pos in range(2):
            key_part = halves(key_rows, key_pos, 0)
            key_seg = halves(segment, key_pos, 0)

            def grow(
                carry,
                key_part=key_part,
                key_seg=key_seg,
                query_part=query_part,
                query_seg=query_seg,
            ):
                old_peak, old_mass = carry
                scores = masked_scores(query_part, key_part, query_seg, key_seg)
                new_peak = jnp.maximum(old_peak, jnp.max(scores, axis=2))
                new_mass = old_mass * jnp.exp(old_peak - new_peak) + jnp.sum(
                    jnp.exp(scores - new_peak[:, :, None]), axis=2
                )
                return (new_peak, new_mass)

            peak, mass = lax.cond(touching(query_seg, key_seg), grow, keep_same, (peak, mass))
        log_norm = peak + jnp.log(mass)
        running = jnp.zeros((span, heads, head_dim), jnp.float32)
        for key_pos in range(2):
            key_part = halves(key_rows, key_pos, 0)
            value_part = halves(value_rows, key_pos, 0)
            key_seg = halves(segment, key_pos, 0)

            def spread(
                carry,
                key_part=key_part,
                value_part=value_part,
                key_seg=key_seg,
                query_part=query_part,
                query_seg=query_seg,
                log_norm=log_norm,
            ):
                scores = masked_scores(query_part, key_part, query_seg, key_seg)
                weights = jnp.exp(scores - log_norm[:, :, None]).astype(jnp.bfloat16)
                return carry + jnp.einsum(
                    "hqk,khd->qhd", weights, value_part, preferred_element_type=jnp.float32
                )

            running = lax.cond(touching(query_seg, key_seg), spread, keep_same, running)
        outputs.append(running)
        norms.append(log_norm)
    return (jnp.concatenate(outputs, axis=0), jnp.concatenate(norms, axis=1))


def attend_backward(packed):
    queries, key_rows, value_rows, segment, log_norm, grad_mixed, attended = packed
    scale = 1.0 / math.sqrt(queries.shape[2])
    row_dot = jnp.sum(grad_mixed * attended, axis=2).T
    query_grads = [jnp.zeros(halves(queries, 0, 0).shape, jnp.float32) for which in range(2)]
    key_grads = [jnp.zeros(halves(queries, 0, 0).shape, jnp.float32) for which in range(2)]
    value_grads = [jnp.zeros(halves(queries, 0, 0).shape, jnp.float32) for which in range(2)]
    for query_pos in range(2):
        query_part = halves(queries, query_pos, 0)
        query_seg = halves(segment, query_pos, 0)
        grad_part = halves(grad_mixed, query_pos, 0)
        norm_part = halves(log_norm, query_pos, 1)
        dot_part = halves(row_dot, query_pos, 1)
        for key_pos in range(2):
            key_part = halves(key_rows, key_pos, 0)
            value_part = halves(value_rows, key_pos, 0)
            key_seg = halves(segment, key_pos, 0)

            def accumulate(
                carry,
                query_part=query_part,
                query_seg=query_seg,
                grad_part=grad_part,
                norm_part=norm_part,
                dot_part=dot_part,
                key_part=key_part,
                value_part=value_part,
                key_seg=key_seg,
            ):
                part_query, part_key, part_value = carry
                scores = masked_scores(query_part, key_part, query_seg, key_seg)
                probs = jnp.exp(scores - norm_part[:, :, None])
                part_value = part_value + jnp.einsum(
                    "hqk,qhd->khd",
                    probs.astype(jnp.bfloat16),
                    grad_part,
                    preferred_element_type=jnp.float32,
                )
                grad_probs = jnp.einsum(
                    "qhd,khd->hqk", grad_part, value_part, preferred_element_type=jnp.float32
                )
                grad_scores = (probs * (grad_probs - dot_part[:, :, None])).astype(jnp.bfloat16)
                part_query = (
                    part_query
                    + jnp.einsum(
                        "hqk,khd->qhd", grad_scores, key_part, preferred_element_type=jnp.float32
                    )
                    * scale
                )
                part_key = (
                    part_key
                    + jnp.einsum(
                        "hqk,qhd->khd", grad_scores, query_part, preferred_element_type=jnp.float32
                    )
                    * scale
                )
                return (part_query, part_key, part_value)

            updated = lax.cond(
                touching(query_seg, key_seg),
                accumulate,
                keep_same,
                (query_grads[query_pos], key_grads[key_pos], value_grads[key_pos]),
            )
            query_grads[query_pos] = updated[0]
            key_grads[key_pos] = updated[1]
            value_grads[key_pos] = updated[2]
    return (
        jnp.concatenate(query_grads, axis=0),
        jnp.concatenate(key_grads, axis=0),
        jnp.concatenate(value_grads, axis=0),
    )


def local(
    frames,
    cotangent,
    segment_ids,
    norm_gain,
    norm_bias,
    w_qkv,
    qv_bias,
    w_out,
    out_bias,
    w_up,
    up_bias,
    w_down,
):
    rows, width = frames.shape
    seq_count, length = segment_ids.shape
    heads = H
    head_dim = width // heads
    shape_four = (seq_count, length, heads, head_dim)
    gathered = (
        lax.all_gather(norm_gain, "shard", axis=1, tiled=True),
        lax.all_gather(norm_bias, "shard", axis=1, tiled=True),
        lax.all_gather(w_qkv, "shard", axis=0, tiled=True),
        lax.all_gather(qv_bias, "shard", axis=1, tiled=True),
        lax.all_gather(w_out, "shard", axis=0, tiled=True),
        lax.all_gather(out_bias, "shard", axis=1, tiled=True),
    )
    gain_full = gathered[0].astype(jnp.float32)
    shift_full = gathered[1].astype(jnp.float32)
    qkv_full = gathered[2]
    qv_full = gathered[3].astype(jnp.float32)
    out_weight = gathered[4]
    outb_full = gathered[5].astype(jnp.float32)
    inputs = frames.astype(jnp.float32)
    unit_one, inverse_one = standardize(inputs)
    normed_one = (unit_one * gain_full[0] + shift_full[0]).astype(jnp.bfloat16)
    projected = jnp.dot(normed_one, qkv_full, preferred_element_type=jnp.float32)
    queries = (projected[:, :width] + qv_full[0]).astype(jnp.bfloat16).reshape(shape_four)
    key_rows = projected[:, width : 2 * width].astype(jnp.bfloat16).reshape(shape_four)
    value_rows = (projected[:, 2 * width :] + qv_full[1]).astype(jnp.bfloat16).reshape(shape_four)
    attended, log_norm = lax.map(attend_forward, (queries, key_rows, value_rows, segment_ids))
    mixed_low = attended.reshape(rows, width).astype(jnp.bfloat16)
    middle = (
        inputs + jnp.dot(mixed_low, out_weight, preferred_element_type=jnp.float32) + outb_full[0]
    )
    unit_two, inverse_two = standardize(middle)
    normed_two = (unit_two * gain_full[1] + shift_full[1]).astype(jnp.bfloat16)
    up_full, upb_full, down_full = (
        lax.all_gather(w_up, "shard", axis=1, tiled=True),
        lax.all_gather(up_bias, "shard", axis=0, tiled=True),
        lax.all_gather(w_down, "shard", axis=0, tiled=True),
    )
    hidden_pre = jnp.dot(normed_two, up_full, preferred_element_type=jnp.float32) + upb_full.astype(
        jnp.float32
    )
    activated = gelu_exact(hidden_pre).astype(jnp.bfloat16)
    branch_two = jnp.dot(activated, down_full, preferred_element_type=jnp.float32)
    result = middle + branch_two + outb_full[1]
    grad_out = cotangent.astype(jnp.float32)
    outb_grad_two = jnp.sum(grad_out, axis=0)
    up_back, down_back = (
        lax.all_gather(w_up, "shard", axis=1, tiled=True),
        lax.all_gather(w_down, "shard", axis=0, tiled=True),
    )
    grad_act = jnp.dot(cotangent, down_back.T, preferred_element_type=jnp.float32)
    grad_hidden = gelu_back(hidden_pre, grad_act).astype(jnp.bfloat16)
    down_grad = jnp.dot(activated.T, cotangent, preferred_element_type=jnp.float32)
    up_grad = jnp.dot(normed_two.T, grad_hidden, preferred_element_type=jnp.float32)
    upb_grad = jnp.sum(grad_hidden, axis=0, dtype=jnp.float32)
    grad_norm_two = jnp.dot(grad_hidden, up_back.T, preferred_element_type=jnp.float32)
    up_local, upb_local, down_local = (
        lax.psum_scatter(
            up_grad.astype(jnp.bfloat16), "shard", scatter_dimension=1, tiled=True
        ).astype(jnp.float32),
        lax.psum_scatter(
            upb_grad.astype(jnp.bfloat16), "shard", scatter_dimension=0, tiled=True
        ).astype(jnp.float32),
        lax.psum_scatter(
            down_grad.astype(jnp.bfloat16), "shard", scatter_dimension=0, tiled=True
        ).astype(jnp.float32),
    )
    up_summed, upb_summed, down_summed = (
        lax.psum(up_local.astype(jnp.bfloat16), "replica").astype(jnp.float32),
        lax.psum(upb_local.astype(jnp.bfloat16), "replica").astype(jnp.float32),
        lax.psum(down_local.astype(jnp.bfloat16), "replica").astype(jnp.float32),
    )
    gain_grad_two = jnp.sum(grad_norm_two * unit_two, axis=0)
    shift_grad_two = jnp.sum(grad_norm_two, axis=0)
    grad_middle = grad_out + norm_back(grad_norm_two * gain_full[1], unit_two, inverse_two)
    grad_branch = grad_middle.astype(jnp.bfloat16)
    outb_grad_one = jnp.sum(grad_branch, axis=0, dtype=jnp.float32)
    qkv_back, out_back = (
        lax.all_gather(w_qkv, "shard", axis=0, tiled=True),
        lax.all_gather(w_out, "shard", axis=0, tiled=True),
    )
    out_grad = jnp.dot(mixed_low.T, grad_branch, preferred_element_type=jnp.float32)
    grad_mixed = jnp.dot(grad_branch, out_back.T, preferred_element_type=jnp.float32).astype(
        jnp.bfloat16
    )
    grad_queries, grad_keys, grad_values = lax.map(
        attend_backward,
        (
            queries,
            key_rows,
            value_rows,
            segment_ids,
            log_norm,
            grad_mixed.reshape(shape_four),
            attended,
        ),
    )
    query_low = grad_queries.reshape(rows, width).astype(jnp.bfloat16)
    key_low = grad_keys.reshape(rows, width).astype(jnp.bfloat16)
    value_low = grad_values.reshape(rows, width).astype(jnp.bfloat16)
    grad_projected = jnp.concatenate([query_low, key_low, value_low], axis=1)
    qv_grad = jnp.stack(
        [
            jnp.sum(query_low, axis=0, dtype=jnp.float32),
            jnp.sum(value_low, axis=0, dtype=jnp.float32),
        ]
    )
    qkv_grad = jnp.dot(normed_one.T, grad_projected, preferred_element_type=jnp.float32)
    grad_norm_one = jnp.dot(grad_projected, qkv_back.T, preferred_element_type=jnp.float32)
    gain_grad_one = jnp.sum(grad_norm_one * unit_one, axis=0)
    shift_grad_one = jnp.sum(grad_norm_one, axis=0)
    grad_inputs = grad_middle + norm_back(grad_norm_one * gain_full[0], unit_one, inverse_one)
    gain_grads = jnp.stack([gain_grad_one, gain_grad_two])
    shift_grads = jnp.stack([shift_grad_one, shift_grad_two])
    outb_grads = jnp.stack([outb_grad_one, outb_grad_two])
    local_grads = (
        lax.psum_scatter(
            gain_grads.astype(jnp.bfloat16), "shard", scatter_dimension=1, tiled=True
        ).astype(jnp.float32),
        lax.psum_scatter(
            shift_grads.astype(jnp.bfloat16), "shard", scatter_dimension=1, tiled=True
        ).astype(jnp.float32),
        lax.psum_scatter(
            qkv_grad.astype(jnp.bfloat16), "shard", scatter_dimension=0, tiled=True
        ).astype(jnp.float32),
        lax.psum_scatter(
            qv_grad.astype(jnp.bfloat16), "shard", scatter_dimension=1, tiled=True
        ).astype(jnp.float32),
        lax.psum_scatter(
            out_grad.astype(jnp.bfloat16), "shard", scatter_dimension=0, tiled=True
        ).astype(jnp.float32),
        lax.psum_scatter(
            outb_grads.astype(jnp.bfloat16), "shard", scatter_dimension=1, tiled=True
        ).astype(jnp.float32),
    )
    summed = (
        lax.psum(local_grads[0].astype(jnp.bfloat16), "replica").astype(jnp.float32),
        lax.psum(local_grads[1].astype(jnp.bfloat16), "replica").astype(jnp.float32),
        lax.psum(local_grads[2].astype(jnp.bfloat16), "replica").astype(jnp.float32),
        lax.psum(local_grads[3].astype(jnp.bfloat16), "replica").astype(jnp.float32),
        lax.psum(local_grads[4].astype(jnp.bfloat16), "replica").astype(jnp.float32),
        lax.psum(local_grads[5].astype(jnp.bfloat16), "replica").astype(jnp.float32),
    )
    return (
        result.astype(jnp.bfloat16),
        grad_inputs,
        summed[0],
        summed[1],
        summed[2],
        summed[3],
        summed[4],
        summed[5],
        up_summed,
        upb_summed,
        down_summed,
    )


def solution(mesh):
    placed = (
        P(("replica", "shard"), None),
        P(("replica", "shard"), None),
        P(("replica", "shard"), None),
        P(None, "shard"),
        P(None, "shard"),
        P("shard", None),
        P(None, "shard"),
        P("shard", None),
        P(None, "shard"),
        P(None, "shard"),
        P("shard"),
        P("shard", None),
    )
    return jax.shard_map(
        local,
        mesh=mesh,
        in_specs=placed,
        out_specs=(
            P(("replica", "shard"), None),
            P(("replica", "shard"), None),
            P(None, "shard"),
            P(None, "shard"),
            P("shard", None),
            P(None, "shard"),
            P("shard", None),
            P(None, "shard"),
            P(None, "shard"),
            P("shard"),
            P("shard", None),
        ),
        check_vma=False,
    )
```

profile of v0, /device:TPU:0, one launch (start us, length us, event | category | flops | bytes accessed | tf_op | source)
XLA Modules:
  0.0 748.9 jit_solution(15768583942616573431)
XLA Ops:
  48.9 13.0 %all-gather.6.cloned.1.call-done = bf16[768,2304]{1,0:T(8,128)(2,1)} async-done(((bf16[384,2304]{1,0:T(8,128)(2,1)}), bf16[768,2304]{1,0:T(8,128)(2,1)}) %all-gather.6.cloned.1.call-update) | async-done | bytes 3538960 | tf_op jit(solution)/shard_map/all_gather | solution.py:211
  61.9 7.9 %fusion.108 = (bf16[1024,2304]{1,0:T(8,128)(2,1)}, f32[1024,2304]{1,0:T(8,128)S(1)}) fusion(bf16[768,2304]{1,0:T(8,128)(2,1)} %all-gather.6.cloned.1.call-done, bf16[1024,768]{0,1:T(8,128)(2,1)S(1)} %copy.79, f32[768]{0:T(1024)S(1)} %get-tuple-element.583, f32[768]{0:T(1024)S(1)} %get-tuple-element.581, f32[1024]{0:T(1024)S(1)} %add_rsqrt_fusion.1, ...), kind=kOutput, calls=%fused_computation.198 | convolution fusion | flops 3630956544 | bytes 19281920 | tf_op jit(solution)/shard_map/dot_general | solution.py:225
  82.3 7.4 conditional.12
  89.7 7.3 conditional.13
  97.8 8.4 %conditional.14 = (f32[512,12,64]{0,2,1:T(8,128)}) conditional(s32[]{:T(128)} %bitcast.14, () %tuple.120, (s32[512]{0:T(512)S(1)}, bf16[512,12,64]{0,2,1:T(8,128)(2,1)S(1)}, bf16[512,12,64]{0,2,1:T(8,128)(2,1)}, f32[12,512]{1,0:T(8,128)S(1)}, bf16[512,12,64]{0,2,1:T(8,128)(2,1)}) %tuple.314), branch_computations={%region_10.11_spmd, %region_11.12_spmd} | conditional | flops 818151424 | bytes 4483080 | solution.py:109
  98.1 8.1 %fusion.6 = f32[512,12,64]{0,2,1:T(8,128)} fusion(bf16[512,12,64]{0,2,1:T(8,128)(2,1)} %get-tuple-element.287, f32[12,512]{1,0:T(8,128)S(1)} %get-tuple-element.286, pred[512,512]{1,0:T(8,128)(4,1)S(1)} %broadcast_compare_fusion.2, bf16[512,12,64]{0,2,1:T(8,128)(2,1)S(1)} %get-tuple-element.284, bf16[512,12,64]{0,2,1:T(8,128)(2,1)} %get-tuple-element.285), kind=kOutput, calls=%fused_computation.15 | convolution fusion | flops 817889280 | bytes 4218880 | tf_op jit(solution)/shard_map/while/body/eval_jaxpr/cond/branch_1_fun/hqk,khd->qhd/dot_general | solution.py:105
  106.2 8.9 %conditional.15 = (f32[512,12,64]{0,2,1:T(8,128)}) conditional(s32[]{:T(128)} %bitcast.13, f32[512,12,64]{0,2,1:T(8,128)} %get-tuple-element.687, (s32[512]{0:T(512)S(1)}, s32[512]{0:T(512)S(1)}, bf16[512,12,64]{0,2,1:T(8,128)(2,1)S(1)}, bf16[512,12,64]{0,2,1:T(8,128)(2,1)S(1)}, f32[12,512]{1,0:T(8,128)S(1)}, ...), branch_computations={%region_12.13_spmd, %region_13.14_spmd} | conditional | flops 818544640 | bytes 6057992 | solution.py:109
  106.8 8.3 %bitcast_add_fusion = f32[512,12,64]{0,2,1:T(8,128)} fusion(f32[512,12,64]{0,2,1:T(8,128)} %get-tuple-element.288, bf16[512,12,64]{0,2,1:T(8,128)(2,1)} %get-tuple-element.294, f32[12,512]{1,0:T(8,128)S(1)} %get-tuple-element.293, pred[512,512]{1,0:T(8,128)(4,1)S(1)} %broadcast_compare_fusion.3, bf16[512,12,64]{0,2,1:T(8,128)(2,1)S(1)} %get-tuple-element.291, ...), kind=kOutput, calls=%fused_computation.23 | convolution fusion | flops 818282496 | bytes 5791744 | tf_op jit(solution)/shard_map/while/body/eval_jaxpr/cond/branch_1_fun/hqk,khd->qhd/dot_general | solution.py:105
  117.4 7.6 %conditional.16 = (f32[12,512]{1,0:T(8,128)}, f32[12,512]{1,0:T(8,128)S(1)}) conditional(s32[]{:T(128)} %bitcast.23, () %tuple.127, (s32[512]{0:T(512)S(1)}, s32[512]{0:T(512)S(1)}, bf16[512,12,64]{0,2,1:T(8,128)(2,1)}, bf16[512,12,64]{0,2,1:T(8,128)(2,1)}) %tuple.316), branch_computations={%region_14.15_spmd, %region_15.0_spmd} | conditional | flops 424953856 | bytes 27725840 | solution.py:86
  125.1 8.4 %conditional.17 = ((f32[12,512]{1,0:T(8,128)}, f32[12,512]{1,0:T(8,128)S(1)})) conditional(s32[]{:T(128)} %bitcast.22, (f32[12,512]{1,0:T(8,128)}, f32[12,512]{1,0:T(8,128)S(1)}) %conditional.16, (s32[512]{0:T(512)S(1)}, bf16[512,12,64]{0,2,1:T(8,128)(2,1)}, bf16[512,12,64]{0,2,1:T(8,128)(2,1)S(1)}, f32[12,512]{1,0:T(8,128)}, ...), branch_computations={%region_18.19_spmd, %region_19.0_spmd} | conditional | flops 424947712 | bytes 27846680 | solution.py:86
  134.2 8.3 %conditional.18 = (f32[512,12,64]{0,2,1:T(8,128)}) conditional(s32[]{:T(128)} %bitcast.23, () %tuple.126, (s32[512]{0:T(512)S(1)}, s32[512]{0:T(512)S(1)}, bf16[512,12,64]{0,2,1:T(8,128)(2,1)}, bf16[512,12,64]{0,2,1:T(8,128)(2,1)S(1)}, f32[12,512]{1,0:T(8,128)S(1)}, /*index=5*/bf16[512,12,64]{0,2,1:T(8,128)(2,1)}) %tuple.317), branch_computations={%region_22.23_spmd, %region_23.24_spmd} | conditional | flops 818151424 | bytes 4485128 | solution.py:109
  134.5 8.0 %fusion.21 = f32[512,12,64]{0,2,1:T(8,128)} fusion(bf16[512,12,64]{0,2,1:T(8,128)(2,1)} %get-tuple-element.309, f32[12,512]{1,0:T(8,128)S(1)} %get-tuple-element.308, pred[512,512]{1,0:T(8,128)(4,1)S(1)} %broadcast_compare_fusion.6, bf16[512,12,64]{0,2,1:T(8,128)(2,1)} %get-tuple-element.306, bf16[512,12,64]{0,2,1:T(8,128)(2,1)S(1)} %get-tuple-element.307), kind=kOutput, calls=%fused_computation.42 | convolution fusion | flops 817889280 | bytes 4218880 | tf_op jit(solution)/shard_map/while/body/eval_jaxpr/cond/branch_1_fun/hqk,khd->qhd/dot_general | solution.py:105
  142.5 9.0 %conditional.19 = (f32[512,12,64]{0,2,1:T(8,128)}) conditional(s32[]{:T(128)} %bitcast.22, f32[512,12,64]{0,2,1:T(8,128)} %get-tuple-element.690, (s32[512]{0:T(512)S(1)}, bf16[512,12,64]{0,2,1:T(8,128)(2,1)}, bf16[512,12,64]{0,2,1:T(8,128)(2,1)S(1)}, f32[12,512]{1,0:T(8,128)S(1)}, bf16[512,12,64]{0,2,1:T(8,128)(2,1)}, ...), branch_computations={%region_24.25_spmd, %region_25.26_spmd} | conditional | flops 818544640 | bytes 6055944 | solution.py:109
  142.9 8.6 %bitcast_add_fusion.1 = f32[512,12,64]{0,2,1:T(8,128)} fusion(f32[512,12,64]{0,2,1:T(8,128)} %get-tuple-element.310, bf16[512,12,64]{0,2,1:T(8,128)(2,1)} %get-tuple-element.315, f32[12,512]{1,0:T(8,128)S(1)} %get-tuple-element.314, pred[512,512]{1,0:T(8,128)(4,1)S(1)} %broadcast_compare_fusion.7, bf16[512,12,64]{0,2,1:T(8,128)(2,1)} %get-tuple-element.312, ...), kind=kOutput, calls=%fused_computation.50 | convolution fusion | flops 818282496 | bytes 5791744 | tf_op jit(solution)/shard_map/while/body/eval_jaxpr/cond/branch_1_fun/hqk,khd->qhd/dot_general | solution.py:105
  159.3 39.0 %multiply_convert_fusion.4 = (bf16[1024,3072]{1,0:T(8,128)(2,1)}, f32[1024,3072]{1,0:T(8,128)}, f32[1024,3072]{1,0:T(8,128)}) fusion(f32[3072]{0:T(1024)S(1)} %bitcast.201, bf16[768,3072]{1,0:T(8,128)(2,1)} %all-gather.10.cloned.1.call-done, f32[1024,768]{0,1:T(8,128)} %copy-done.8, f32[768]{0:T(1024)S(1)} %get-tuple-element.582, ...), kind=kOutput, calls=%fused_computation.101 | convolution fusion | flops 5043388416 | bytes 39348224 | tf_op jit(solution)/shard_map/dot_general | solution.py:241
  198.3 16.4 %all-gather.12.cloned.1.call-done = bf16[3072,768]{1,0:T(8,128)(2,1)} async-done(((bf16[1536,768]{1,0:T(8,128)(2,1)}), bf16[3072,768]{1,0:T(8,128)(2,1)}) %all-gather.12.cloned.1.call-update) | async-done | bytes 4718608 | tf_op jit(solution)/shard_map/all_gather | solution.py:239
  214.6 17.3 %fusion.112 = (bf16[3072]{0:T(1024)(128)(2,1)}, bf16[1024,3072]{1,0:T(8,128)(2,1)}) fusion(f32[1024,3072]{1,0:T(8,128)} %get-tuple-element.602, bf16[1024,768]{1,0:T(8,128)(2,1)S(1)} %copy-done.23, bf16[3072,768]{1,0:T(8,128)(2,1)} %all-gather.12.cloned.1.call-done, f32[1024,3072]{1,0:T(8,128)} %get-tuple-element.633, f32[3072]{0:T(1024)S(1)} %bitcast.202), kind=kOutput, calls=%fused_computation.202 | convolution fusion | flops 4882166784 | bytes 37767168 | tf_op jit(solution)/shard_map/dot_general | solution.py:253
  232.0 10.5 %fusion.110 = (bf16[768]{0:T(1024)(128)(2,1)}, f32[1024,768]{1,0:T(8,128)}) fusion(bf16[1024,3072]{1,0:T(8,128)(2,1)} %get-tuple-element.639, bf16[768,3072]{1,0:T(8,128)(2,1)} %all-gather.10.cloned.1.call-done), kind=kOutput, calls=%fused_computation.200 | convolution fusion | flops 4832623616 | bytes 14157312 | tf_op jit(solution)/shard_map/dot_general | solution.py:258
  260.8 14.6 %conditional.20 = (f32[512,12,64]{0,2,1:T(8,128)}, f32[512,12,64]{0,2,1:T(8,128)S(1)}, f32[512,12,64]{0,2,1:T(8,128)S(1)}) conditional(s32[]{:T(128)} %bitcast.14, () %tuple.132, (s32[512]{0:T(512)S(1)}, bf16[512,12,64]{0,2,1:T(8,128)(2,1)S(1)}, bf16[512,12,64]{0,2,1:T(8,128)(2,1)S(1)}, f32[12,512]{1,0:T(8,128)S(1)}, ...), branch_computations={%region_31.32_spmd.clone, %region_32.33_spmd.clone} | conditional | flops 2045771776 | bytes 77146216 | solution.py:173
  277.1 16.9 %conditional.21 = (f32[512,12,64]{0,2,1:T(8,128)}, f32[512,12,64]{0,2,1:T(8,128)S(1)}, f32[512,12,64]{0,2,1:T(8,128)}) conditional(s32[]{:T(128)} %bitcast.13, f32[512,12,64]{0,2,1:T(8,128)} %get-tuple-element.394, (s32[512]{0:T(512)S(1)}, s32[512]{0:T(512)S(1)}, bf16[512,12,64]{0,2,1:T(8,128)(2,1)S(1)}, bf16[512,12,64]{0,2,1:T(8,128)(2,1)S(1)}, ...), branch_computations={%region_33.34_spmd, %region_34.35_spmd} | conditional | flops 2046164992 | bytes 75575376 | solution.py:173
  295.2 18.5 %conditional.22 = (f32[512,12,64]{0,2,1:T(8,128)}, f32[512,12,64]{0,2,1:T(8,128)}, f32[512,12,64]{0,2,1:T(8,128)}) conditional(s32[]{:T(128)} %bitcast.23, (f32[512,12,64]{0,2,1:T(8,128)}, f32[512,12,64]{0,2,1:T(8,128)}) %tuple.289, (s32[512]{0:T(512)S(1)}, s32[512]{0:T(512)S(1)}, bf16[512,12,64]{0,2,1:T(8,128)(2,1)}, ...), branch_computations={%region_35.36_spmd, %region_36.37_spmd} | conditional | flops 2046558208 | bytes 105459936 | solution.py:173
  313.7 21.3 %conditional.23 = (f32[512,12,64]{0,2,1:T(8,128)}, f32[512,12,64]{0,2,1:T(8,128)}, f32[512,12,64]{0,2,1:T(8,128)}) conditional(s32[]{:T(128)} %bitcast.22, (f32[512,12,64]{0,2,1:T(8,128)}, f32[512,12,64]{0,2,1:T(8,128)}, f32[512,12,64]{0,2,1:T(8,128)}) %tuple.287, (s32[512]{0:T(512)S(1)}, bf16[512,12,64]{0,2,1:T(8,128)(2,1)}, ...), branch_computations={%region_37.38_spmd, %region_38.39_spmd} | conditional | flops 2046951424 | bytes 91302032 | solution.py:173
  349.2 9.7 %convolution_convert_fusion.1 = bf16[768,3072]{1,0:T(8,128)(2,1)} fusion(bf16[1024,3072]{1,0:T(8,128)(2,1)} %get-tuple-element.639, f32[1024,768]{0,1:T(8,128)} %copy-done.8, f32[768]{0:T(1024)S(1)} %copy-done.68, f32[768]{0:T(1024)S(1)} %get-tuple-element.580, f32[1024]{0:T(1024)S(1)} %add_rsqrt_fusion, f32[1024]{0:T(1024)S(1)} %broadcast_multiply_fusion.4), kind=kOutput, calls=%fused_computation.116 | convolution fusion | flops 4838129664 | bytes 14170112 | tf_op jit(solution)/shard_map/dot_general | solution.py:256
  360.3 9.6 %convolution_convert_fusion = bf16[3072,768]{1,0:T(8,128)(2,1)} fusion(bf16[1024,3072]{1,0:T(8,128)(2,1)} %get-tuple-element.601, bf16[1024,768]{1,0:T(8,128)(2,1)S(1)} %copy-done.24), kind=kOutput, calls=%fused_computation.115 | convolution fusion | flops 4834197504 | bytes 12582912 | tf_op jit(solution)/shard_map/dot_general | solution.py:255
  371.4 9.0 %fusion.111 = (bf16[768]{0:T(1024)(128)(2,1)S(1)}, f32[1024,768]{1,0:T(8,128)}) fusion(bf16[768,2304]{1,0:T(8,128)(2,1)} %all-gather.6.cloned.1.call-done, bf16[1024,768]{0,1:T(8,128)(2,1)} %bitcast.159, bf16[1024,768]{0,1:T(8,128)(2,1)} %bitcast.155, bf16[1024,768]{0,1:T(8,128)(2,1)} %bitcast.157), kind=kOutput, calls=%fused_computation.201 | convolution fusion | flops 3638820096 | bytes 11404800 | tf_op jit(solution)/shard_map/dot_general | solution.py:311
  397.0 62.9 %reduce-scatter.21.cloned.1.call-done = bf16[768,1536]{1,0:T(8,128)(2,1)} async-done(((bf16[768,3072]{1,0:T(8,128)(2,1)}), bf16[768,1536]{1,0:T(8,128)(2,1)}) %reduce-scatter.21.cloned.1.call-update) | async-done | bytes 2359312 | tf_op jit(solution)/shard_map/reduce_scatter | solution.py:260
  459.8 63.0 %reduce-scatter.23.cloned.1.call-done = bf16[1536,768]{1,0:T(8,128)(2,1)} async-done(((bf16[3072,768]{1,0:T(8,128)(2,1)}), bf16[1536,768]{1,0:T(8,128)(2,1)}) %reduce-scatter.23.cloned.1.call-update) | async-done | bytes 2359312 | tf_op jit(solution)/shard_map/reduce_scatter | solution.py:266
  533.4 9.5 %add_convert_fusion.1 = bf16[1024,768]{0,1:T(8,128)(2,1)} fusion(f32[1024,768]{0,1:T(8,128)S(1)} %copy-done.10, bf16[1024,3072]{1,0:T(8,128)(2,1)} %get-tuple-element.601, bf16[3072,768]{1,0:T(8,128)(2,1)} %all-gather.12.cloned.1.call-done, f32[768]{0:T(1024)S(1)} %copy-done.66), kind=kOutput, calls=%fused_computation.149 | convolution fusion | flops 4834197504 | bytes 15731712 | tf_op jit(solution)/shard_map/dot_general | solution.py:245
  552.5 9.8 %reduce-scatter.25.cloned.1.call-done = bf16[384,2]{1,0:T(8,128)(2,1)} async-done(((bf16[768,2]{1,0:T(8,128)(2,1)}), bf16[384,2]{1,0:T(8,128)(2,1)}) %reduce-scatter.25.cloned.1.call-update) | async-done | bytes 1552
  563.3 12.1 %reduce-scatter.31.cloned.1.call-done = bf16[384,2]{1,0:T(8,128)(2,1)} async-done(((bf16[768,2]{1,0:T(8,128)(2,1)}), bf16[384,2]{1,0:T(8,128)(2,1)}) %reduce-scatter.31.cloned.1.call-update) | async-done | bytes 1552
  576.4 64.0 %all-reduce.1 = (bf16[2,384]{1,0:T(2,128)(2,1)S(1)}, bf16[2,384]{1,0:T(2,128)(2,1)S(1)}, bf16[2,384]{1,0:T(2,128)(2,1)S(1)}, bf16[2,384]{1,0:T(2,128)(2,1)S(1)}, bf16[1536]{0:T(1024)(128)(2,1)S(1)}) all-reduce(bf16[2,384]{1,0:T(2,128)(2,1)S(1)} %copy.96, ...), channel_id=1, replica_groups=mesh['replica'=16,'shard'=2] {'replica'}, use_global_device_ids=true, to_apply=%region_44.45 | all-reduce | flops 4608 | bytes 18432 | tf_op jit(solution)/shard_map/psum | solution.py:339
  643.4 88.3 %all-reduce.5.cloned.1.call-done = (bf16[384,2304]{1,0:T(8,128)(2,1)}, bf16[384,768]{1,0:T(8,128)(2,1)}, bf16[768,1536]{1,0:T(8,128)(2,1)}, bf16[1536,768]{1,0:T(8,128)(2,1)}) async-done(((bf16[384,2304]{1,0:T(8,128)(2,1)}, bf16[384,768]{1,0:T(8,128)(2,1)}, bf16[768,1536]{1,0:T(8,128)(2,1)}, bf16[1536,768]{1,0:T(8,128)(2,1)}), (bf16[384,2304]{1,0:T(8,128)(2,1)}, bf16[384,768]{1,0:T(8,128)(2,1)}, ...) | async-done | bytes 7077904 | tf_op jit(solution)/shard_map/psum | solution.py:341
  (335 shorter events, 245.3 us)
Async XLA Ops:
  7.2 54.7 %all-gather.6.cloned.1.call-start = ((), (), s32[]{:S(2)}) async-start(), calls=%async_computation.8 | async-start | bytes 5308416 | tf_op jit(solution)/shard_map/all_gather | solution.py:211
  7.9 145.7 %all-gather.8.cloned.1.call-start = ((), (), s32[]{:S(2)}) async-start(), calls=%async_computation.9 | async-start | bytes 1769472 | tf_op jit(solution)/shard_map/all_gather | solution.py:213
  8.7 150.6 %all-gather.10.cloned.1.call-start = ((), (), s32[]{:S(2)}) async-start(), calls=%async_computation.10 | async-start | bytes 7077888 | tf_op jit(solution)/shard_map/all_gather | solution.py:237
  9.4 19.6 %copy-start.74 = (bf16[2,384]{1,0:T(2,128)(2,1)S(1)}, bf16[2,384]{1,0:T(2,128)(2,1)}, u32[]{:S(2)}) copy-start(bf16[2,384]{1,0:T(2,128)(2,1)} %param.40) | copy-start | bytes 4612
  9.4 24.0 %copy-start.75 = (bf16[2,384]{1,0:T(2,128)(2,1)S(1)}, bf16[2,384]{1,0:T(2,128)(2,1)}, u32[]{:S(2)}) copy-start(bf16[2,384]{1,0:T(2,128)(2,1)} %param.42) | copy-start | bytes 4612
  9.4 28.4 %copy-start.76 = (bf16[2,384]{1,0:T(2,128)(2,1)S(1)}, bf16[2,384]{1,0:T(2,128)(2,1)}, u32[]{:S(2)}) copy-start(bf16[2,384]{1,0:T(2,128)(2,1)} %param.44) | copy-start | bytes 4612
  9.4 33.4 %copy-start.71 = (bf16[1536]{0:T(1024)(128)(2,1)S(1)}, bf16[1536]{0:T(1024)(128)(2,1)}, u32[]{:S(2)}) copy-start(bf16[1536]{0:T(1024)(128)(2,1)} %param.46) | copy-start | bytes 9220
  9.5 37.9 %copy-start.22 = (bf16[1024,768]{1,0:T(8,128)(2,1)S(1)}, bf16[1024,768]{1,0:T(8,128)(2,1)}, u32[]{:S(2)}) copy-start(bf16[1024,768]{1,0:T(8,128)(2,1)} %param.37) | copy-start | bytes 4718596
  9.5 205.2 %all-gather.12.cloned.1.call-start = ((), (), s32[]{:S(2)}) async-start(), calls=%async_computation.11 | async-start | bytes 7077888 | tf_op jit(solution)/shard_map/all_gather | solution.py:239
  10.0 380.0 %reduce-scatter.19.cloned.1.call-start = ((), (), s32[]{:S(2)}) async-start(), calls=%async_computation.13 | async-start | bytes 1769472 | tf_op jit(solution)/shard_map/reduce_scatter | solution.py:331
  10.1 124.1 %copy-start.51 = (s32[1,512]{1,0:T(1,128)}, s32[1,512]{1,0:T(1,128)S(1)}, u32[]{:S(2)}) copy-start(s32[1,512]{1,0:T(1,128)S(1)} %get-tuple-element.623) | copy-start | bytes 6148
  10.1 132.4 %copy-start.49 = (s32[1,512]{1,0:T(1,128)}, s32[1,512]{1,0:T(1,128)S(1)}, u32[]{:S(2)}) copy-start(s32[1,512]{1,0:T(1,128)S(1)} %get-tuple-element.624) | copy-start | bytes 6148
  22.9 130.8 %copy-start.2 = (bf16[1024,768]{0,1:T(8,128)(2,1)}, bf16[1024,768]{0,1:T(8,128)(2,1)S(1)}, u32[]{:S(2)}) copy-start(bf16[1024,768]{0,1:T(8,128)(2,1)S(1)} %copy.79) | copy-start | bytes 4718596
  23.2 46.6 %copy-start.53 = (f32[1024]{0:T(1024)}, f32[1024]{0:T(1024)S(1)}, u32[]{:S(2)}) copy-start(f32[1024]{0:T(1024)S(1)} %broadcast_multiply_fusion.5) | copy-start | bytes 12292
  23.7 46.2 %copy-start.57 = (f32[1024]{0:T(1024)}, f32[1024]{0:T(1024)S(1)}, u32[]{:S(2)}) copy-start(f32[1024]{0:T(1024)S(1)} %add_rsqrt_fusion.1) | copy-start | bytes 12292
  29.0 40.8 %copy-start.55 = (f32[768]{0:T(1024)}, f32[768]{0:T(1024)S(1)}, u32[]{:S(2)}) copy-start(f32[768]{0:T(1024)S(1)} %get-tuple-element.581) | copy-start | bytes 9220
  33.4 36.4 %copy-start.69 = (f32[768]{0:T(1024)}, f32[768]{0:T(1024)S(1)}, u32[]{:S(2)}) copy-start(f32[768]{0:T(1024)S(1)} %get-tuple-element.583) | copy-start | bytes 9220
  33.4 125.8 %copy-start.67 = (f32[768]{0:T(1024)}, f32[768]{0:T(1024)S(1)}, u32[]{:S(2)}) copy-start(f32[768]{0:T(1024)S(1)} %get-tuple-element.582) | copy-start | bytes 9220
  72.2 34.0 %copy-start = (bf16[512,768]{0,1:T(8,128)(2,1)}, bf16[512,768]{0,1:T(8,128)(2,1)S(1)}, u32[]{:S(2)}) copy-start(bf16[512,768]{0,1:T(8,128)(2,1)S(1)} %copy.80) | copy-start | bytes 2359300
  77.4 65.1 %copy-start.4 = (bf16[512,768]{0,1:T(8,128)(2,1)}, bf16[512,768]{0,1:T(8,128)(2,1)S(1)}, u32[]{:S(2)}) copy-start(bf16[512,768]{0,1:T(8,128)(2,1)S(1)} %copy.82) | copy-start | bytes 2359300
  159.3 55.3 %copy-start.23 = (bf16[1024,768]{1,0:T(8,128)(2,1)S(1)}, bf16[1024,768]{1,0:T(8,128)(2,1)}, u32[]{:S(2)}) copy-start(bf16[1024,768]{1,0:T(8,128)(2,1)} %param.37) | copy-start | bytes 4718596
  255.3 141.6 %reduce-scatter.17.cloned.1.call-start = ((), (), s32[]{:S(2)}) async-start(), calls=%async_computation.12 | async-start | bytes 5308416 | tf_op jit(solution)/shard_map/reduce_scatter | solution.py:325
  275.5 18.5 %copy-start.62 = (f32[12,512]{1,0:T(8,128)S(1)}, f32[12,512]{1,0:T(8,128)}, u32[]{:S(2)}) copy-start(f32[12,512]{1,0:T(8,128)} %copy-done.61) | copy-start | bytes 73732
  313.7 22.8 %copy-start.15 = (f32[512,12,64]{0,2,1:T(8,128)S(1)}, f32[512,12,64]{0,2,1:T(8,128)}, u32[]{:S(2)}) copy-start(f32[512,12,64]{0,2,1:T(8,128)} %get-tuple-element.403) | copy-start | bytes 4718596
  349.1 110.7 %reduce-scatter.21.cloned.1.call-start = ((), (), s32[]{:S(2)}) async-start(), calls=%async_computation.14 | async-start | bytes 7077888 | tf_op jit(solution)/shard_map/reduce_scatter | solution.py:260
  358.9 163.9 %reduce-scatter.23.cloned.1.call-start = ((), (), s32[]{:S(2)}) async-start(), calls=%async_computation.15 | async-start | bytes 7077888 | tf_op jit(solution)/shard_map/reduce_scatter | solution.py:266
  370.0 180.6 %reduce-scatter.29.cloned.1.call-start = ((), (), s32[]{:S(2)}) async-start(), calls=%async_computation.18 | async-start | bytes 294912
  386.9 136.0 %copy-start.78 = (u32[32]{0:T(128)S(1)}, u32[32]{0:T(128)}, u32[]{:S(2)}) copy-start(u32[32]{0:T(128)} %constant.209) | copy-start | bytes 388
  386.9 164.6 %reduce-scatter.27.cloned.1.call-start = ((), (), s32[]{:S(2)}) async-start(), calls=%async_computation.17 | async-start | bytes 294912
  387.9 174.5 %reduce-scatter.25.cloned.1.call-start = ((), (), s32[]{:S(2)}) async-start(), calls=%async_computation.16 | async-start | bytes 294912
  388.8 186.6 %reduce-scatter.31.cloned.1.call-start = ((), (), s32[]{:S(2)}) async-start(), calls=%async_computation.19 | async-start | bytes 294912
  389.8 341.9 %all-reduce.5.cloned.1.call-start = ((), (), s32[]{:S(2)}) async-start(), calls=%async_computation.20 | async-start | bytes 14155776 | tf_op jit(solution)/shard_map/psum | solution.py:341
  (60 other events, 270.2 us)
Sparse Core Ops, SparseCore 0:
  9.6 52.3 all-gather.5
  63.5 22.7 all-gather.7
  87.8 62.6 all-gather.9
  151.9 62.6 all-gather.11
  255.4 21.7 reduce-scatter.18
  349.3 47.6 reduce-scatter.16
  399.8 59.9 reduce-scatter.20
  462.8 60.0 reduce-scatter.22
  525.1 10.9 reduce-scatter.28
  538.2 10.9 reduce-scatter.26
  551.4 10.9 reduce-scatter.24
  564.5 10.9 reduce-scatter.30
  579.5 152.0 all-reduce.4
where the time goes:
time: 759 us; the launch traced here: 749 us
  waiting for transfers between devices  275 us (36%)
  matrix products  241 us (32%)
  blocking collectives  91.8 us (12%)
  other arithmetic  58.7 us (8%)
  local copies, waits for them, and re-layouts  52.9 us (7%)
  between operations  26.3 us (3%)
    psum x1, waiting for transfers between devices, local(): lax.psum(local_grads[2].astype(jnp.bfloat16), 'replica').astype(jnp.float32)  88.3 us
    psum x1, blocking collectives, local(): lax.psum(local_grads[0].astype(jnp.bfloat16), 'replica').astype(jnp.float32)  64 us
    reduce_scatter x1, waiting for transfers between devices, local(): lax.psum_scatter(down_grad.astype(jnp.bfloat16), 'shard', scatter_dimensi...  63 us
    reduce_scatter x1, waiting for transfers between devices, local(): lax.psum_scatter(up_grad.astype(jnp.bfloat16), 'shard', scatter_dimension...  62.9 us
    dot_general x1, matrix products, local(): jnp.dot(normed_two, up_full, preferred_element_type=jnp.float32)  39 us
    dot_general x4, matrix products, spread(): jnp.einsum('hqk,khd->qhd', weights, value_part, preferred_element_type=jn...  33 us
    unnamed x141, local copies, waits for them, and re-layouts  26.3 us
    unnamed x17, waiting for transfers between devices  24.7 us
  transfers between devices with their start and end apart: 13, of which 8 were waited for; matrix products, arithmetic and copies ran while one was open for 39% of the time, Pallas kernels for 0%

commit v1 on v0

--- a/solution.py
+++ b/solution.py
@@ -338,7 +338,9 @@
     summed = (
         lax.psum(local_grads[0].astype(jnp.bfloat16), "replica").astype(jnp.float32),
         lax.psum(local_grads[1].astype(jnp.bfloat16), "replica").astype(jnp.float32),
-        lax.psum(local_grads[2].astype(jnp.bfloat16), "replica").astype(jnp.float32),
+        jnp.sum(lax.all_gather(local_grads[2].astype(jnp.bfloat16), "replica"), axis=0).astype(
+            jnp.float32
+        ),
         lax.psum(local_grads[3].astype(jnp.bfloat16), "replica").astype(jnp.float32),
         lax.psum(local_grads[4].astype(jnp.bfloat16), "replica").astype(jnp.float32),
         lax.psum(local_grads[5].astype(jnp.bfloat16), "replica").astype(jnp.float32),

time: 759 us -> 811 us (1.069)
  waiting for transfers between devices: 275 us -> 326 us
  other arithmetic: 58.7 us -> 70.3 us
  matrix products: 241 us -> 230 us
    all_gather x0 -> x1, waiting for transfers between devices: none -> 135 us  [local(): lax.all_gather(local_grads[2].astype(jnp.bfloat16), 'replica')]
    reduce_scatter x1, waiting for transfers between devices: 62.9 us -> 0.02 us  [local(): lax.psum_scatter(up_grad.astype(jnp.bfloat16), 'shard', scatter_dimension...]
    reduce_scatter x1, waiting for transfers between devices: 63 us -> 18.4 us  [local(): lax.psum_scatter(down_grad.astype(jnp.bfloat16), 'shard', scatter_dimensi...]
    reduce_scatter x1, waiting for transfers between devices: 6.87 us -> 50.6 us  [local(): lax.psum_scatter(qkv_grad.astype(jnp.bfloat16), 'shard', scatter_dimensio...]
    psum x1, waiting for transfers between devices: 88.3 us -> 63.1 us  [local(): lax.psum(local_grads[4].astype(jnp.bfloat16), 'replica').astype(jnp.float32)]
    reduce_sum x0 -> x1, other arithmetic: none -> 10.2 us  [local(): jnp.sum(lax.all_gather(local_grads[2].astype(jnp.bfloat16), 'replica'), a...]
    unnamed x17 -> x18, waiting for transfers between devices: 24.7 us -> 26.4 us
    unnamed x141 -> x135, local copies, waits for them, and re-layouts: 26.3 us -> 27.2 us
  transfers between devices with their start and end apart: 13 -> 14, of which waited for: 8 -> 8; matrix products, arithmetic and copies ran while one was open for 39% -> 36% of each run, Pallas kernels for 0% -> 0%
where the time goes in v1:
time: 811 us; the launch traced here: 801 us
  waiting for transfers between devices  326 us (40%)
  matrix products  230 us (28%)
  blocking collectives  91 us (11%)
  other arithmetic  70.3 us (9%)
  local copies, waits for them, and re-layouts  54.9 us (7%)
  between operations  26.1 us (3%)
    all_gather x1, waiting for transfers between devices, local(): lax.all_gather(local_grads[2].astype(jnp.bfloat16), 'replica')  135 us
    psum x1, blocking collectives, local(): lax.psum(local_grads[0].astype(jnp.bfloat16), 'replica').astype(jnp.float32)  63.3 us
    psum x1, waiting for transfers between devices, local(): lax.psum(local_grads[4].astype(jnp.bfloat16), 'replica').astype(jnp.float32)  63.1 us
    reduce_scatter x1, waiting for transfers between devices, local(): lax.psum_scatter(qkv_grad.astype(jnp.bfloat16), 'shard', scatter_dimensio...  50.6 us
    dot_general x1, matrix products, local(): jnp.dot(normed_two, up_full, preferred_element_type=jnp.float32)  38.9 us
    dot_general x4, matrix products, spread(): jnp.einsum('hqk,khd->qhd', weights, value_part, preferred_element_type=jn...  32.8 us
    unnamed x135, local copies, waits for them, and re-layouts  27.2 us
    unnamed x18, waiting for transfers between devices  26.4 us
  transfers between devices with their start and end apart: 14, of which 8 were waited for; matrix products, arithmetic and copies ran while one was open for 36% of the time, Pallas kernels for 0%

profile of v1, /device:TPU:0, one launch (start us, length us, event | category | flops | bytes accessed | tf_op | source)
XLA Modules:
  0.0 800.8 jit_solution(3456188086604275943)
XLA Ops:
  48.8 13.1 %all-gather.8.cloned.1.call-done = bf16[768,2304]{1,0:T(8,128)(2,1)} async-done(((bf16[384,2304]{1,0:T(8,128)(2,1)}), bf16[768,2304]{1,0:T(8,128)(2,1)}) %all-gather.8.cloned.1.call-update) | async-done | bytes 3538960 | tf_op jit(solution)/shard_map/all_gather | solution.py:211
  62.0 7.9 fusion.108
  97.9 8.4 %conditional.18 = (f32[512,12,64]{0,2,1:T(8,128)}) conditional(s32[]{:T(128)} %bitcast.23, () %tuple.126, (s32[512]{0:T(512)S(1)}, s32[512]{0:T(512)S(1)}, bf16[512,12,64]{0,2,1:T(8,128)(2,1)S(1)}, bf16[512,12,64]{0,2,1:T(8,128)(2,1)}, f32[12,512]{1,0:T(8,128)S(1)}, /*index=5*/bf16[512,12,64]{0,2,1:T(8,128)(2,1)}) %tuple.321), branch_computations={%region_22.23_spmd, %region_23.24_spmd} | conditional | flops 818151424 | bytes 4485128 | solution.py:109
  98.1 8.1 %fusion.21 = f32[512,12,64]{0,2,1:T(8,128)} fusion(bf16[512,12,64]{0,2,1:T(8,128)(2,1)} %get-tuple-element.309, f32[12,512]{1,0:T(8,128)S(1)} %get-tuple-element.308, pred[512,512]{1,0:T(8,128)(4,1)S(1)} %broadcast_compare_fusion.6, bf16[512,12,64]{0,2,1:T(8,128)(2,1)S(1)} %get-tuple-element.306, bf16[512,12,64]{0,2,1:T(8,128)(2,1)} %get-tuple-element.307), kind=kOutput, calls=%fused_computation.42 | convolution fusion | flops 817889280 | bytes 4218880 | tf_op jit(solution)/shard_map/while/body/eval_jaxpr/cond/branch_1_fun/hqk,khd->qhd/dot_general | solution.py:105
  106.2 8.7 %conditional.19 = (f32[512,12,64]{0,2,1:T(8,128)}) conditional(s32[]{:T(128)} %bitcast.22, f32[512,12,64]{0,2,1:T(8,128)} %get-tuple-element.688, (s32[512]{0:T(512)S(1)}, bf16[512,12,64]{0,2,1:T(8,128)(2,1)S(1)}, bf16[512,12,64]{0,2,1:T(8,128)(2,1)S(1)}, f32[12,512]{1,0:T(8,128)S(1)}, bf16[512,12,64]{0,2,1:T(8,128)(2,1)}, ...), branch_computations={%region_24.25_spmd, %region_25.26_spmd} | conditional | flops 818544640 | bytes 6055944 | solution.py:109
  106.6 8.3 %bitcast_add_fusion.1 = f32[512,12,64]{0,2,1:T(8,128)} fusion(f32[512,12,64]{0,2,1:T(8,128)} %get-tuple-element.310, bf16[512,12,64]{0,2,1:T(8,128)(2,1)} %get-tuple-element.315, f32[12,512]{1,0:T(8,128)S(1)} %get-tuple-element.314, pred[512,512]{1,0:T(8,128)(4,1)S(1)} %broadcast_compare_fusion.7, bf16[512,12,64]{0,2,1:T(8,128)(2,1)S(1)} %get-tuple-element.312, ...), kind=kOutput, calls=%fused_computation.50 | convolution fusion | flops 818282496 | bytes 5791744 | tf_op jit(solution)/shard_map/while/body/eval_jaxpr/cond/branch_1_fun/hqk,khd->qhd/dot_general | solution.py:105
  116.4 7.4 conditional.12
  123.8 7.5 conditional.13
  132.1 8.3 %conditional.14 = (f32[512,12,64]{0,2,1:T(8,128)}) conditional(s32[]{:T(128)} %bitcast.14, () %tuple.120, (s32[512]{0:T(512)S(1)}, bf16[512,12,64]{0,2,1:T(8,128)(2,1)S(1)}, bf16[512,12,64]{0,2,1:T(8,128)(2,1)}, f32[12,512]{1,0:T(8,128)S(1)}, bf16[512,12,64]{0,2,1:T(8,128)(2,1)}) %tuple.324), branch_computations={%region_10.11_spmd, %region_11.12_spmd} | conditional | flops 818151424 | bytes 4483080 | solution.py:109
  132.3 8.0 %fusion.6 = f32[512,12,64]{0,2,1:T(8,128)} fusion(bf16[512,12,64]{0,2,1:T(8,128)(2,1)} %get-tuple-element.287, f32[12,512]{1,0:T(8,128)S(1)} %get-tuple-element.286, pred[512,512]{1,0:T(8,128)(4,1)S(1)} %broadcast_compare_fusion.2, bf16[512,12,64]{0,2,1:T(8,128)(2,1)S(1)} %get-tuple-element.284, bf16[512,12,64]{0,2,1:T(8,128)(2,1)} %get-tuple-element.285), kind=kOutput, calls=%fused_computation.15 | convolution fusion | flops 817889280 | bytes 4218880 | tf_op jit(solution)/shard_map/while/body/eval_jaxpr/cond/branch_1_fun/hqk,khd->qhd/dot_general | solution.py:105
  140.4 8.7 %conditional.15 = (f32[512,12,64]{0,2,1:T(8,128)}) conditional(s32[]{:T(128)} %bitcast.13, f32[512,12,64]{0,2,1:T(8,128)} %get-tuple-element.685, (s32[512]{0:T(512)S(1)}, s32[512]{0:T(512)S(1)}, bf16[512,12,64]{0,2,1:T(8,128)(2,1)S(1)}, bf16[512,12,64]{0,2,1:T(8,128)(2,1)S(1)}, f32[12,512]{1,0:T(8,128)S(1)}, ...), branch_computations={%region_12.13_spmd, %region_13.14_spmd} | conditional | flops 818544640 | bytes 6057992 | solution.py:109
  140.8 8.3 %bitcast_add_fusion = f32[512,12,64]{0,2,1:T(8,128)} fusion(f32[512,12,64]{0,2,1:T(8,128)} %get-tuple-element.288, bf16[512,12,64]{0,2,1:T(8,128)(2,1)} %get-tuple-element.294, f32[12,512]{1,0:T(8,128)S(1)} %get-tuple-element.293, pred[512,512]{1,0:T(8,128)(4,1)S(1)} %broadcast_compare_fusion.3, bf16[512,12,64]{0,2,1:T(8,128)(2,1)S(1)} %get-tuple-element.291, ...), kind=kOutput, calls=%fused_computation.23 | convolution fusion | flops 818282496 | bytes 5791744 | tf_op jit(solution)/shard_map/while/body/eval_jaxpr/cond/branch_1_fun/hqk,khd->qhd/dot_general | solution.py:105
  156.9 38.9 %multiply_convert_fusion.4 = (bf16[1024,3072]{1,0:T(8,128)(2,1)}, f32[1024,3072]{1,0:T(8,128)}, f32[1024,3072]{1,0:T(8,128)}) fusion(f32[3072]{0:T(1024)S(1)} %bitcast.209, bf16[768,3072]{1,0:T(8,128)(2,1)} %all-gather.12.cloned.1.call-done, f32[1024,768]{0,1:T(8,128)} %copy-done.9, f32[768]{0:T(1024)S(1)} %get-tuple-element.582, ...), kind=kOutput, calls=%fused_computation.101 | convolution fusion | flops 5043388416 | bytes 39348224 | tf_op jit(solution)/shard_map/dot_general | solution.py:241
  195.8 18.8 %all-gather.14.cloned.1.call-done = bf16[3072,768]{1,0:T(8,128)(2,1)} async-done(((bf16[1536,768]{1,0:T(8,128)(2,1)}), bf16[3072,768]{1,0:T(8,128)(2,1)}) %all-gather.14.cloned.1.call-update) | async-done | bytes 4718608 | tf_op jit(solution)/shard_map/all_gather | solution.py:239
  214.6 17.3 %fusion.112 = (bf16[3072]{0:T(1024)(128)(2,1)}, bf16[1024,3072]{1,0:T(8,128)(2,1)}) fusion(f32[1024,3072]{1,0:T(8,128)} %get-tuple-element.601, bf16[1024,768]{1,0:T(8,128)(2,1)S(1)} %copy-done.24, bf16[3072,768]{1,0:T(8,128)(2,1)} %all-gather.14.cloned.1.call-done, f32[1024,3072]{1,0:T(8,128)} %get-tuple-element.632, f32[3072]{0:T(1024)S(1)} %bitcast.210), kind=kOutput, calls=%fused_computation.202 | convolution fusion | flops 4882166784 | bytes 37767168 | tf_op jit(solution)/shard_map/dot_general | solution.py:253
  232.0 10.7 %fusion.110 = (bf16[768]{0:T(1024)(128)(2,1)}, f32[1024,768]{1,0:T(8,128)}) fusion(bf16[1024,3072]{1,0:T(8,128)(2,1)} %get-tuple-element.638, bf16[768,3072]{1,0:T(8,128)(2,1)} %all-gather.12.cloned.1.call-done), kind=kOutput, calls=%fused_computation.200 | convolution fusion | flops 4832623616 | bytes 14157312 | tf_op jit(solution)/shard_map/dot_general | solution.py:258
  255.6 9.7 %convolution_convert_fusion.1 = bf16[768,3072]{1,0:T(8,128)(2,1)} fusion(bf16[1024,3072]{1,0:T(8,128)(2,1)} %get-tuple-element.638, f32[1024,768]{0,1:T(8,128)S(1)} %copy-done.10, f32[768]{0:T(1024)S(1)} %get-tuple-element.582, f32[768]{0:T(1024)S(1)} %get-tuple-element.580, f32[1024]{0:T(1024)S(1)} %add_rsqrt_fusion, f32[1024]{0:T(1024)S(1)} %broadcast_multiply_fusion.4), kind=kOutput, calls=%fused_computation.116 | convolution fusion | flops 4838129664 | bytes 14170112 | tf_op jit(solution)/shard_map/dot_general | solution.py:256
  266.8 9.7 %convolution_convert_fusion = bf16[3072,768]{1,0:T(8,128)(2,1)} fusion(bf16[1024,3072]{1,0:T(8,128)(2,1)} %get-tuple-element.600, bf16[1024,768]{1,0:T(8,128)(2,1)S(1)} %copy-done.25), kind=kOutput, calls=%fused_computation.115 | convolution fusion | flops 4834197504 | bytes 12582912 | tf_op jit(solution)/shard_map/dot_general | solution.py:255
  283.3 14.5 %conditional.20 = (f32[512,12,64]{0,2,1:T(8,128)}, f32[512,12,64]{0,2,1:T(8,128)S(1)}, f32[512,12,64]{0,2,1:T(8,128)S(1)}) conditional(s32[]{:T(128)} %bitcast.14, () %tuple.132, (s32[512]{0:T(512)S(1)}, bf16[512,12,64]{0,2,1:T(8,128)(2,1)S(1)}, bf16[512,12,64]{0,2,1:T(8,128)(2,1)S(1)}, f32[12,512]{1,0:T(8,128)S(1)}, ...), branch_computations={%region_31.32_spmd.clone, %region_32.33_spmd.clone} | conditional | flops 2045771776 | bytes 74000464 | solution.py:173
  299.4 17.1 %conditional.21 = (f32[512,12,64]{0,2,1:T(8,128)}, f32[512,12,64]{0,2,1:T(8,128)S(1)}, f32[512,12,64]{0,2,1:T(8,128)}) conditional(s32[]{:T(128)} %bitcast.13, f32[512,12,64]{0,2,1:T(8,128)} %get-tuple-element.394, (s32[512]{0:T(512)S(1)}, s32[512]{0:T(512)S(1)}, bf16[512,12,64]{0,2,1:T(8,128)(2,1)S(1)}, bf16[512,12,64]{0,2,1:T(8,128)(2,1)S(1)}, ...), branch_computations={%region_33.34_spmd, %region_34.35_spmd} | conditional | flops 2046164992 | bytes 78721128 | solution.py:173
  317.7 15.4 %conditional.22 = (f32[512,12,64]{0,2,1:T(8,128)S(1)}, f32[512,12,64]{0,2,1:T(8,128)}, f32[512,12,64]{0,2,1:T(8,128)}) conditional(s32[]{:T(128)} %bitcast.23, (f32[512,12,64]{0,2,1:T(8,128)}, f32[512,12,64]{0,2,1:T(8,128)}) %tuple.297, (s32[512]{0:T(512)S(1)}, s32[512]{0:T(512)S(1)}, bf16[512,12,64]{0,2,1:T(8,128)(2,1)S(1)}, ...), branch_computations={%region_35.36_spmd, %region_36.37_spmd} | conditional | flops 2046558208 | bytes 105459936 | solution.py:173
  333.1 17.4 %conditional.23 = (f32[512,12,64]{0,2,1:T(8,128)S(1)}, f32[512,12,64]{0,2,1:T(8,128)}, f32[512,12,64]{0,2,1:T(8,128)}) conditional(s32[]{:T(128)} %bitcast.22, (f32[512,12,64]{0,2,1:T(8,128)S(1)}, f32[512,12,64]{0,2,1:T(8,128)}, f32[512,12,64]{0,2,1:T(8,128)}) %tuple.295, (s32[512]{0:T(512)S(1)}, bf16[512,12,64]{0,2,1:T(8,128)(2,1)S(1)}, ...), branch_computations={%region_37.38_spmd, %region_38.39_spmd} | conditional | flops 2046951424 | bytes 91302032 | solution.py:173
  364.9 9.1 %fusion.111 = (bf16[768]{0:T(1024)(128)(2,1)S(1)}, f32[1024,768]{1,0:T(8,128)}) fusion(bf16[768,2304]{1,0:T(8,128)(2,1)} %all-gather.8.cloned.1.call-done, bf16[1024,768]{0,1:T(8,128)(2,1)} %bitcast.167, bf16[1024,768]{0,1:T(8,128)(2,1)} %bitcast.163, bf16[1024,768]{0,1:T(8,128)(2,1)} %bitcast.169), kind=kOutput, calls=%fused_computation.201 | convolution fusion | flops 3638820096 | bytes 11404800 | tf_op jit(solution)/shard_map/dot_general | solution.py:311
  384.8 18.4 %reduce-scatter.23.cloned.1.call-done = bf16[1536,768]{1,0:T(8,128)(2,1)} async-done(((bf16[3072,768]{1,0:T(8,128)(2,1)}), bf16[1536,768]{1,0:T(8,128)(2,1)}) %reduce-scatter.23.cloned.1.call-update) | async-done | bytes 2359312 | tf_op jit(solution)/shard_map/reduce_scatter | solution.py:266
  403.3 50.6 %reduce-scatter.17.cloned.1.call-done = bf16[384,2304]{1,0:T(8,128)(2,1)} async-done(((bf16[768,2304]{1,0:T(8,128)(2,1)}), bf16[384,2304]{1,0:T(8,128)(2,1)}) %reduce-scatter.17.cloned.1.call-update) | async-done | bytes 1769488 | tf_op jit(solution)/shard_map/reduce_scatter | solution.py:325
  455.1 9.1 %add_convert_fusion.1 = bf16[1024,768]{0,1:T(8,128)(2,1)S(1)} fusion(f32[1024,768]{0,1:T(8,128)} %copy-done.9, bf16[1024,3072]{1,0:T(8,128)(2,1)} %get-tuple-element.600, bf16[3072,768]{1,0:T(8,128)(2,1)} %all-gather.14.cloned.1.call-done, f32[768]{0:T(1024)S(1)} %copy-done.66), kind=kOutput, calls=%fused_computation.149 | convolution fusion | flops 4834197504 | bytes 15731712 | tf_op jit(solution)/shard_map/dot_general | solution.py:245
  481.9 11.5 %reduce-scatter.29.cloned.1.call-done = bf16[384,2]{1,0:T(8,128)(2,1)} async-done(((bf16[768,2]{1,0:T(8,128)(2,1)}), bf16[384,2]{1,0:T(8,128)(2,1)}) %reduce-scatter.29.cloned.1.call-update) | async-done | bytes 1552
  494.4 12.1 %reduce-scatter.31.cloned.1.call-done = bf16[384,2]{1,0:T(8,128)(2,1)} async-done(((bf16[768,2]{1,0:T(8,128)(2,1)}), bf16[384,2]{1,0:T(8,128)(2,1)}) %reduce-scatter.31.cloned.1.call-update) | async-done | bytes 1552
  507.5 63.3 %all-reduce.1 = (bf16[2,384]{1,0:T(2,128)(2,1)S(1)}, bf16[2,384]{1,0:T(2,128)(2,1)S(1)}, bf16[2,384]{1,0:T(2,128)(2,1)S(1)}, bf16[2,384]{1,0:T(2,128)(2,1)S(1)}, bf16[1536]{0:T(1024)(128)(2,1)S(1)}) all-reduce(bf16[2,384]{1,0:T(2,128)(2,1)S(1)} %copy.96, ...), channel_id=1, replica_groups=mesh['replica'=16,'shard'=2] {'replica'}, use_global_device_ids=true, to_apply=%region_44.45 | all-reduce | flops 4608 | bytes 18432 | tf_op jit(solution)/shard_map/psum | solution.py:339
  573.7 63.1 %all-reduce.5.cloned.1.call-done = (bf16[384,768]{1,0:T(8,128)(2,1)}, bf16[768,1536]{1,0:T(8,128)(2,1)}, bf16[1536,768]{1,0:T(8,128)(2,1)}) async-done(((bf16[384,768]{1,0:T(8,128)(2,1)}, bf16[768,1536]{1,0:T(8,128)(2,1)}, bf16[1536,768]{1,0:T(8,128)(2,1)}), (bf16[384,768]{1,0:T(8,128)(2,1)}, bf16[768,1536]{1,0:T(8,128)(2,1)}, bf16[1536,768]{1,0:T(8,128)(2,1)})) %all-reduce.5.cloned.1.call-update) | async-done | bytes 5308432 | tf_op jit(solution)/shard_map/psum | solution.py:345
  646.7 135.1 %all-gather.16.cloned.1.call-done = bf16[6144,2304]{1,0:T(8,128)(2,1)} async-done(((bf16[384,2304]{1,0:T(8,128)(2,1)}), bf16[6144,2304]{1,0:T(8,128)(2,1)}) %all-gather.16.cloned.1.call-update) | async-done | bytes 28311568 | tf_op jit(solution)/shard_map/all_gather | solution.py:341
  781.9 10.2 %reduce_sum.227 = bf16[384,2304]{1,0:T(8,128)(2,1)S(1)} reduce(bf16[16,384,2304]{2,1,0:T(8,128)(2,1)} %bitcast.160, bf16[]{:T(256)} %constant.202.clone.1), dimensions={0}, to_apply=%region_50.51 | reduce | flops 13271040 | bytes 30081026 | tf_op jit(solution)/shard_map/reduce_sum | solution.py:341
  (333 shorter events, 245.2 us)
Async XLA Ops:
  7.2 21.5 %copy-start.72 = (bf16[2,384]{1,0:T(2,128)(2,1)S(1)}, bf16[2,384]{1,0:T(2,128)(2,1)}, u32[]{:S(2)}) copy-start(bf16[2,384]{1,0:T(2,128)(2,1)} %param.40) | copy-start | bytes 4612
  7.2 54.7 %all-gather.8.cloned.1.call-start = ((), (), s32[]{:S(2)}) async-start(), calls=%async_computation.8 | async-start | bytes 5308416 | tf_op jit(solution)/shard_map/all_gather | solution.py:211
  7.9 25.2 %copy-start.73 = (bf16[2,384]{1,0:T(2,128)(2,1)S(1)}, bf16[2,384]{1,0:T(2,128)(2,1)}, u32[]{:S(2)}) copy-start(bf16[2,384]{1,0:T(2,128)(2,1)} %param.39) | copy-start | bytes 4612
  8.0 143.4 %all-gather.10.cloned.1.call-start = ((), (), s32[]{:S(2)}) async-start(), calls=%async_computation.9 | async-start | bytes 1769472 | tf_op jit(solution)/shard_map/all_gather | solution.py:213
  8.7 148.2 %all-gather.12.cloned.1.call-start = ((), (), s32[]{:S(2)}) async-start(), calls=%async_computation.10 | async-start | bytes 7077888 | tf_op jit(solution)/shard_map/all_gather | solution.py:237
  9.4 28.8 %copy-start.74 = (bf16[2,384]{1,0:T(2,128)(2,1)S(1)}, bf16[2,384]{1,0:T(2,128)(2,1)}, u32[]{:S(2)}) copy-start(bf16[2,384]{1,0:T(2,128)(2,1)} %param.42) | copy-start | bytes 4612
  9.4 33.2 %copy-start.69 = (bf16[1536]{0:T(1024)(128)(2,1)S(1)}, bf16[1536]{0:T(1024)(128)(2,1)}, u32[]{:S(2)}) copy-start(bf16[1536]{0:T(1024)(128)(2,1)} %param.46) | copy-start | bytes 9220
  9.5 37.7 %copy-start.23 = (bf16[1024,768]{1,0:T(8,128)(2,1)S(1)}, bf16[1024,768]{1,0:T(8,128)(2,1)}, u32[]{:S(2)}) copy-start(bf16[1024,768]{1,0:T(8,128)(2,1)} %param.37) | copy-start | bytes 4718596
  9.5 205.2 %all-gather.14.cloned.1.call-start = ((), (), s32[]{:S(2)}) async-start(), calls=%async_computation.11 | async-start | bytes 7077888 | tf_op jit(solution)/shard_map/all_gather | solution.py:239
  10.0 374.8 %reduce-scatter.19.cloned.1.call-start = ((), (), s32[]{:S(2)}) async-start(), calls=%async_computation.13 | async-start | bytes 1769472 | tf_op jit(solution)/shard_map/reduce_scatter | solution.py:331
  13.3 127.1 %copy-start.49 = (s32[1,512]{1,0:T(1,128)}, s32[1,512]{1,0:T(1,128)S(1)}, u32[]{:S(2)}) copy-start(s32[1,512]{1,0:T(1,128)S(1)} %get-tuple-element.623) | copy-start | bytes 6148
  13.3 127.1 %copy-start.51 = (s32[1,512]{1,0:T(1,128)}, s32[1,512]{1,0:T(1,128)S(1)}, u32[]{:S(2)}) copy-start(s32[1,512]{1,0:T(1,128)S(1)} %get-tuple-element.622) | copy-start | bytes 6148
  28.7 122.6 %copy-start.2 = (bf16[1024,768]{0,1:T(8,128)(2,1)}, bf16[1024,768]{0,1:T(8,128)(2,1)S(1)}, u32[]{:S(2)}) copy-start(bf16[1024,768]{0,1:T(8,128)(2,1)S(1)} %copy.79) | copy-start | bytes 4718596
  33.1 36.7 %copy-start.67 = (f32[768]{0:T(1024)}, f32[768]{0:T(1024)S(1)}, u32[]{:S(2)}) copy-start(f32[768]{0:T(1024)S(1)} %get-tuple-element.583) | copy-start | bytes 9220
  37.5 32.3 %copy-start.55 = (f32[768]{0:T(1024)}, f32[768]{0:T(1024)S(1)}, u32[]{:S(2)}) copy-start(f32[768]{0:T(1024)S(1)} %get-tuple-element.581) | copy-start | bytes 9220
  37.8 32.0 %copy-start.53 = (f32[1024]{0:T(1024)}, f32[1024]{0:T(1024)S(1)}, u32[]{:S(2)}) copy-start(f32[1024]{0:T(1024)S(1)} %broadcast_multiply_fusion.5) | copy-start | bytes 12292
  38.3 31.6 %copy-start.57 = (f32[1024]{0:T(1024)}, f32[1024]{0:T(1024)S(1)}, u32[]{:S(2)}) copy-start(f32[1024]{0:T(1024)S(1)} %add_rsqrt_fusion.1) | copy-start | bytes 12292
  72.2 34.0 %copy-start.4 = (bf16[512,768]{0,1:T(8,128)(2,1)}, bf16[512,768]{0,1:T(8,128)(2,1)S(1)}, u32[]{:S(2)}) copy-start(bf16[512,768]{0,1:T(8,128)(2,1)S(1)} %copy.85) | copy-start | bytes 2359300
  77.5 62.9 %copy-start.6 = (bf16[512,768]{0,1:T(8,128)(2,1)}, bf16[512,768]{0,1:T(8,128)(2,1)S(1)}, u32[]{:S(2)}) copy-start(bf16[512,768]{0,1:T(8,128)(2,1)S(1)} %copy.82) | copy-start | bytes 2359300
  116.4 24.0 %copy-start = (bf16[512,768]{0,1:T(8,128)(2,1)}, bf16[512,768]{0,1:T(8,128)(2,1)S(1)}, u32[]{:S(2)}) copy-start(bf16[512,768]{0,1:T(8,128)(2,1)S(1)} %copy.80) | copy-start | bytes 2359300
  156.9 57.8 %copy-start.24 = (bf16[1024,768]{1,0:T(8,128)(2,1)S(1)}, bf16[1024,768]{1,0:T(8,128)(2,1)}, u32[]{:S(2)}) copy-start(bf16[1024,768]{1,0:T(8,128)(2,1)} %param.37) | copy-start | bytes 4718596
  255.6 129.3 %reduce-scatter.21.cloned.1.call-start = ((), (), s32[]{:S(2)}) async-start(), calls=%async_computation.14 | async-start | bytes 7077888 | tf_op jit(solution)/shard_map/reduce_scatter | solution.py:260
  265.4 137.8 %reduce-scatter.23.cloned.1.call-start = ((), (), s32[]{:S(2)}) async-start(), calls=%async_computation.15 | async-start | bytes 7077888 | tf_op jit(solution)/shard_map/reduce_scatter | solution.py:266
  276.5 177.4 %reduce-scatter.17.cloned.1.call-start = ((), (), s32[]{:S(2)}) async-start(), calls=%async_computation.12 | async-start | bytes 5308416 | tf_op jit(solution)/shard_map/reduce_scatter | solution.py:325
  364.4 115.6 %reduce-scatter.25.cloned.1.call-start = ((), (), s32[]{:S(2)}) async-start(), calls=%async_computation.17 | async-start | bytes 294912
  380.7 73.2 %copy-start.75 = (u32[32]{0:T(128)S(1)}, u32[32]{0:T(128)}, u32[]{:S(2)}) copy-start(u32[32]{0:T(128)} %constant.210) | copy-start | bytes 388
  380.7 74.4 %copy-start.66 = (f32[768]{0:T(1024)S(1)}, f32[768]{0:T(1024)}, u32[]{:S(2)}) copy-start(f32[768]{0:T(1024)} %get-tuple-element.578) | copy-start | bytes 9220
  381.7 99.2 %reduce-scatter.27.cloned.1.call-start = ((), (), s32[]{:S(2)}) async-start(), calls=%async_computation.18 | async-start | bytes 294912
  382.8 110.6 %reduce-scatter.29.cloned.1.call-start = ((), (), s32[]{:S(2)}) async-start(), calls=%async_computation.19 | async-start | bytes 294912
  383.8 122.7 %reduce-scatter.31.cloned.1.call-start = ((), (), s32[]{:S(2)}) async-start(), calls=%async_computation.20 | async-start | bytes 294912
  384.7 252.1 %all-reduce.5.cloned.1.call-start = ((), (), s32[]{:S(2)}) async-start(), calls=%async_computation.21 | async-start | bytes 10616832 | tf_op jit(solution)/shard_map/psum | solution.py:345
  403.2 378.6 %all-gather.16.cloned.1.call-start = ((), (), s32[]{:S(2)}) async-start(), calls=%async_computation.16 | async-start | bytes 30081024 | tf_op jit(solution)/shard_map/all_gather | solution.py:341
  (58 other events, 255.4 us)
Sparse Core Ops, SparseCore 0:
  9.6 52.3 all-gather.7
  63.5 22.7 all-gather.9
  87.9 62.6 all-gather.11
  151.9 62.6 all-gather.13
  255.7 21.7 reduce-scatter.18
  280.3 59.9 reduce-scatter.20
  343.2 59.9 reduce-scatter.22
  406.1 47.6 reduce-scatter.16
  456.1 10.9 reduce-scatter.24
  469.1 11.0 reduce-scatter.26
  482.4 10.9 reduce-scatter.28
  495.5 10.9 reduce-scatter.30
  510.6 126.2 all-reduce.4
  638.4 143.4 all-gather.15
